TPU v7x, 32 devices: a whole 2x2x4 slice. The times are simulated.
32 devices in a mesh: row: 2 (over y), col: 4 (over z), mp: 4 (over x, core).
Axes of the slice: x: 2, y: 2, z: 4, core: 2. Of those that a mesh axis runs over, the one named last changes fastest.
Arguments:
- hidden: bfloat16 [8192, 3584], P(('row', 'col'), 'mp'), may hold values from -6 to 6
- old_logp: float32 [8192], P(('row', 'col')), may hold values from -0.6 to 0.6
- rewards: float32 [64], P(('row', 'col')), may hold values from -4 to 4
- resp_dest: int32 [64], P(('row', 'col')), may hold values from 0 to 7, as said below
- resp_len: int32 [64], P(('row', 'col')), may hold values from 1 to 128, as said below
- resp_offset: int32 [64], P(('row', 'col')), may hold values from 0 to 511, as said below
- prompt_group: int32 [64], P(('row', 'col')), may hold values from 0 to 7, as said below
- attn_gain: bfloat16 [3584], replicated, may hold values from 0.099609375 to 1.8984375
- w_query: bfloat16 [3584, 3584], P(None, 'mp'), may hold values from -0.09375 to 0.09375
- q_bias: bfloat16 [3584], P('mp'), may hold values from -3 to 3
- w_key: bfloat16 [3584, 512], P(None, 'mp'), may hold values from -0.09375 to 0.09375
- k_bias: bfloat16 [512], P('mp'), may hold values from -6 to 6
- w_value: bfloat16 [3584, 512], P(None, 'mp'), may hold values from -0.09375 to 0.09375
- v_bias: bfloat16 [512], P('mp'), may hold values from -3 to 3
- w_out: bfloat16 [3584, 3584], P('mp'), may hold values from -0.5 to 0.5
- final_gain: bfloat16 [3584], replicated, may hold values from 0.099609375 to 1.8984375
- chosen_rows: bfloat16 [4096, 3584], P(('row', 'col', 'mp')), may hold values from -0.01171875 to 0.01171875
- log_normalizer: float32 [4096], P(('row', 'col', 'mp')), may hold values from -0.6 to 0.6
Outputs:
- objective: float32 [4096], P(('row', 'col', 'mp'))
- loss: float32 [], replicated
Inputs may be any that keep to these rules, and one draw needn't show every extreme that they name: `resp_dest`: ranks are numbered row index * 4 + col index. A rank's responses go to ranks of the same col index: exactly 4 of them to each such rank, itself included; so every rank receives exactly 8 responses. `resp_len`: the responses bound for one rank hold at most 512 tokens together; in every draw some rank's responses fill all 512 positions, and some response has exactly 128. `resp_offset`: responses bound for one rank lie end to end from position 0, without gaps or intersection. `prompt_group`: each of the 8 groups has exactly 8 responses.
All inputs are finite; a program needn't handle non-finite values.
Results may differ from a plain program's by a relative error of at most 0.0019.
Values may be sent and summed in bfloat16 or wider, within the bound.
A program may use at most 128 MiB of HBM per device.

v0:
```python
import jax
import jax.numpy as jnp
from jax import lax
from jax.sharding import PartitionSpec as P

HEAD = 128
GROUP_SIZE = 8
norm_eps = 1e-06
rope_theta = 1000000.0
clip_low = 0.2
clip_high = 0.28
std_floor = 1.0
mask_fill = -1e30


def rotary(matrix, positions):
    half_size = matrix.shape[-1] // 2
    exponents = jnp.arange(half_size, dtype=jnp.float32) * (2.0 / matrix.shape[-1])
    frequency = rope_theta ** (-exponents)
    angles = positions[:, None] * frequency[None, :]
    cosine_table = jnp.cos(angles)[:, None, :]
    sine_table = jnp.sin(angles)[:, None, :]
    first_half = matrix[..., :half_size]
    second_half = matrix[..., half_size:]
    return jnp.concatenate(
        [
            first_half * cosine_table - second_half * sine_table,
            second_half * cosine_table + first_half * sine_table,
        ],
        -1,
    )


def body(
    hidden,
    old_logp,
    rewards,
    resp_dest,
    resp_len,
    resp_offset,
    prompt_group,
    attn_gain,
    w_query,
    q_bias,
    w_key,
    k_bias,
    w_value,
    v_bias,
    w_out,
    final_gain,
    chosen_rows,
    log_normalizer,
):
    highest = lax.Precision.HIGHEST
    row_ranks = lax.axis_size("row")
    col_ranks = lax.axis_size("col")
    rank_count = row_ranks * col_ranks
    response_count = resp_dest.shape[0]
    per_peer = response_count // row_ranks
    group_count = rank_count * response_count // GROUP_SIZE
    slot_length = hidden.shape[0] // response_count
    feature_count = hidden.shape[1]
    pack_length = response_count * slot_length // 2
    shard_count = lax.axis_size("mp")
    row_count = pack_length // shard_count
    slot_iota = jnp.arange(response_count, dtype=jnp.int32)
    group_iota = jnp.arange(group_count, dtype=jnp.int32)
    dest_row = resp_dest // col_ranks
    earlier = (slot_iota[None, :] < slot_iota[:, None]) & (dest_row[None, :] == dest_row[:, None])
    slot_in_peer = jnp.sum(earlier.astype(jnp.int32), 1)
    send_slot = dest_row * per_peer + slot_in_peer
    selector = send_slot[None, :] == slot_iota[:, None]
    selector_wide = selector.astype(jnp.float32)
    send_rows = jnp.dot(
        selector.astype(jnp.bfloat16),
        hidden.reshape(response_count, slot_length * feature_count),
        preferred_element_type=jnp.float32,
    ).astype(jnp.bfloat16)
    send_rows = send_rows.reshape(row_ranks, per_peer * slot_length, feature_count)
    send_logp = jnp.dot(
        selector_wide, old_logp.reshape(response_count, slot_length), precision=highest
    )
    send_logp = send_logp.reshape(row_ranks, per_peer * slot_length)
    send_length = jnp.dot(selector_wide, resp_len.astype(jnp.float32), precision=highest)
    send_offset = jnp.dot(selector_wide, resp_offset.astype(jnp.float32), precision=highest)
    member = (prompt_group[:, None] == group_iota[None, :]).astype(jnp.float32)
    totals, squares = lax.psum(
        (
            jnp.dot(rewards, member, precision=highest),
            jnp.dot(rewards * rewards, member, precision=highest),
        ),
        ("row", "col"),
    )
    means = totals / GROUP_SIZE
    variance = jnp.maximum(squares / GROUP_SIZE - means * means, 0.0)
    means, scales = (means, jnp.maximum(jnp.sqrt(variance), std_floor))
    member_adv = (rewards - jnp.dot(member, means, precision=highest)) / jnp.dot(
        member, scales, precision=highest
    )
    send_info = jnp.stack(
        [send_length, send_offset, jnp.dot(selector_wide, member_adv, precision=highest)], 1
    )
    send_info = send_info.reshape(row_ranks, per_peer, send_info.shape[1])
    recv_rows = lax.all_to_all(send_rows, "row", split_axis=0, concat_axis=0, tiled=True)
    recv_logp, recv_info = (
        lax.all_to_all(send_logp, "row", split_axis=0, concat_axis=0, tiled=True),
        lax.all_to_all(send_info, "row", split_axis=0, concat_axis=0, tiled=True),
    )
    recv_info = recv_info.reshape(response_count, recv_info.shape[2])
    lengths = recv_info[:, 0].astype(jnp.int32)
    offsets = recv_info[:, 1].astype(jnp.int32)
    slots = jnp.arange(pack_length, dtype=jnp.int32)[:, None]
    covered = (slots >= offsets[None, :]) & (slots < (offsets + lengths)[None, :])
    occupied = jnp.any(covered, 1)
    within_all = slots - offsets[None, :]
    token_index = jnp.sum(jnp.where(covered, slot_iota[None, :] * slot_length + within_all, 0), 1)
    positions = jnp.sum(jnp.where(covered, within_all, 0), 1).astype(jnp.float32)
    segment = jnp.where(occupied, jnp.sum(jnp.where(covered, slot_iota[None, :], 0), 1), -1)
    flat_rows = recv_rows.reshape(-1, feature_count)
    all_rows = lax.all_gather(flat_rows, "mp", axis=1, tiled=True)
    gathered = jnp.where(occupied[:, None], all_rows[token_index], jnp.zeros((), jnp.bfloat16))
    inverse = lax.rsqrt(
        jnp.mean(jnp.square(gathered.astype(jnp.float32)), -1, keepdims=True) + norm_eps
    )
    normed = (gathered.astype(jnp.float32) * inverse * attn_gain.astype(jnp.float32)).astype(
        jnp.bfloat16
    )
    heads_local = w_query.shape[1] // HEAD
    key_heads = w_key.shape[1] // HEAD
    queries = jnp.dot(normed, w_query, preferred_element_type=jnp.float32) + q_bias.astype(
        jnp.float32
    )
    queries = rotary(queries.reshape(pack_length, heads_local, HEAD), positions).astype(
        jnp.bfloat16
    )
    key_rows = jnp.dot(normed, w_key, preferred_element_type=jnp.float32) + k_bias.astype(
        jnp.float32
    )
    key_rows = rotary(key_rows.reshape(pack_length, key_heads, HEAD), positions).astype(
        jnp.bfloat16
    )
    value_rows = (
        (jnp.dot(normed, w_value, preferred_element_type=jnp.float32) + v_bias.astype(jnp.float32))
        .astype(jnp.bfloat16)
        .reshape(pack_length, key_heads, HEAD)
    )
    grouped = queries.reshape(pack_length, key_heads, heads_local // key_heads, HEAD)
    block_size = min(512, pack_length)
    scores = jnp.einsum(
        "qkgd,ekd->kgqe", grouped, key_rows, preferred_element_type=jnp.float32
    ) * HEAD ** (-0.5)
    allowed = (segment[0:block_size, None] == segment[None, :block_size]) & (
        jnp.arange(block_size)[None, :] <= jnp.arange(0, block_size)[:, None]
    )
    scores = jnp.where(allowed, scores, mask_fill)
    highest_score = jnp.max(scores, -1, keepdims=True)
    exponent = jnp.exp(scores - highest_score)
    weights = (exponent / jnp.sum(exponent, -1, keepdims=True)).astype(jnp.bfloat16)
    block_out = jnp.einsum(
        "kgqe,ekd->qkgd", weights, value_rows, preferred_element_type=jnp.float32
    )
    pieces = block_out.reshape(block_size, heads_local * HEAD).astype(jnp.bfloat16)
    branch = lax.psum_scatter(
        jnp.dot(pieces, w_out, preferred_element_type=jnp.float32).astype(jnp.bfloat16),
        "mp",
        scatter_dimension=0,
        tiled=True,
    ).astype(jnp.float32)
    own_start = lax.axis_index("mp") * row_count
    residual = lax.dynamic_slice_in_dim(gathered, own_start, row_count, 0)
    residual_out = (residual.astype(jnp.float32) + branch).astype(jnp.bfloat16)
    final_rows = residual_out.astype(jnp.float32)
    final_inverse = lax.rsqrt(jnp.mean(final_rows * final_rows, -1, keepdims=True) + norm_eps)
    logits = jnp.sum(
        final_rows
        * final_inverse
        * final_gain.astype(jnp.float32)
        * chosen_rows.astype(jnp.float32),
        -1,
    )
    own_covered = lax.dynamic_slice_in_dim(covered, own_start, row_count, 0)
    own_occupied = lax.dynamic_slice_in_dim(occupied, own_start, row_count, 0)
    own_token = lax.dynamic_slice_in_dim(token_index, own_start, row_count, 0)
    own_old = jnp.where(own_occupied, recv_logp.reshape(-1)[own_token], 0.0)
    pair_adv = recv_info[:, 2]
    token_adv = jnp.sum(jnp.where(own_covered, pair_adv[None, :], 0.0), 1)
    ratios = jnp.exp(logits - log_normalizer - own_old)
    bounded = jnp.clip(ratios, 1.0 - clip_low, 1.0 + clip_high)
    objective = jnp.where(own_occupied, jnp.minimum(ratios * token_adv, bounded * token_adv), 0.0)
    loss_sum, counted = lax.psum(
        (jnp.sum(objective), jnp.sum(own_occupied.astype(jnp.float32))), ("row", "col", "mp")
    )
    return (objective, -loss_sum / counted)


def solution(mesh):
    return jax.shard_map(
        body,
        mesh=mesh,
        in_specs=(
            P(("row", "col"), "mp"),
            P(("row", "col")),
            P(("row", "col")),
            P(("row", "col")),
            P(("row", "col")),
            P(("row", "col")),
            P(("row", "col")),
            P(),
            P(None, "mp"),
            P("mp"),
            P(None, "mp"),
            P("mp"),
            P(None, "mp"),
            P("mp"),
            P("mp", None),
            P(),
            P(("row", "col", "mp"), None),
            P(("row", "col", "mp")),
        ),
        out_specs=(P(("row", "col", "mp")), P()),
        check_vma=False,
    )
```

profile of v0, /device:TPU:0, one launch (start us, length us, event | category | flops | bytes accessed | tf_op | source)
XLA Modules:
  0.0 247.5 jit_solution(9806434673147270967)
XLA Ops:
  8.8 2.3 reshape.259
  11.2 1.9 convolution_convert_fusion
  13.0 2.3 reshape.260
  15.5 27.1 %all_to_all.19 = bf16[2,512,896]{2,1,0:T(8,128)(2,1)} all-to-all(bf16[2,512,896]{2,1,0:T(8,128)(2,1)S(1)} %reshape.260), channel_id=1, replica_groups=mesh['row'=2,'col'=4,'mp'=4] {'row'}, dimensions={0} | all-to-all | bytes 3670016 | tf_op jit(solution)/shard_map/all_to_all | solution.py:104
  43.0 20.7 %all-reduce.1 = (f32[8]{0:T(128)S(1)}, f32[8]{0:T(128)S(1)}) all-reduce(f32[8]{0:T(128)S(1)} %convolution_bitcast_fusion.2, f32[8]{0:T(128)S(1)} %convolution_bitcast_fusion.4), channel_id=1, replica_groups=mesh['row'=2,'col'=4,'mp'=4] {'row','col'}, use_global_device_ids=true, to_apply=%region_2.3 | all-reduce | flops 16 | bytes 128 | tf_op jit(solution)/shard_map/psum | solution.py:87
  65.3 3.2 %all-to-all-start = ((f32[2,4,3]{1,2,0:T(4,128)}), f32[2,4,3]{1,2,0:T(4,128)S(1)}, u32[]{:S(2)}, u32[]{:S(2)}) async-start(f32[2,4,3]{1,2,0:T(4,128)} %copy.38), calls=%async_computation | async-start | bytes 8192 | tf_op jit(solution)/shard_map/all_to_all | solution.py:107
  69.2 3.1 %all-to-all-done = f32[2,4,3]{1,2,0:T(4,128)S(1)} async-done(((f32[2,4,3]{1,2,0:T(4,128)}), f32[2,4,3]{1,2,0:T(4,128)S(1)}, u32[]{:S(2)}, u32[]{:S(2)}) %all-to-all-start) | async-done | bytes 128 | tf_op jit(solution)/shard_map/all_to_all | solution.py:107
  75.5 20.0 %all-gather.2.cloned.1.call-done = bf16[1024,3584]{1,0:T(8,128)(2,1)} async-done(((bf16[1024,896]{1,0:T(8,128)(2,1)}), bf16[1024,3584]{1,0:T(8,128)(2,1)}) %all-gather.2.cloned.1.call-update) | async-done | bytes 7340048 | tf_op jit(solution)/shard_map/all_gather | solution.py:120
  95.5 12.1 %gather_fusion = bf16[512,3584]{1,0:T(8,128)(2,1)} fusion(bf16[1024,3584]{1,0:T(8,128)(2,1)} %all-gather.2.cloned.1.call-done, s32[1024]{0:T(1024)S(1)} %pad_clamp_fusion.1), kind=kCustom, calls=%fused_computation | custom fusion | bytes 7342080 | tf_op jit(solution)/shard_map/gather | solution.py:121
  107.6 3.4 %fusion = (f32[512]{0:T(512)S(1)}, bf16[512,3584]{1,0:T(8,128)(2,1)S(1)}) fusion(bf16[512,3584]{1,0:T(8,128)(2,1)} %gather_fusion, pred[512]{0:T(512)(128)(4,1)S(1)} %get-tuple-element.23), kind=kLoop, calls=%fused_computation.5 | loop fusion | flops 7339520 | bytes 7342592 | tf_op jit(solution)/shard_map/reduce_sum | solution.py:123
  114.0 5.3 %convolution_add_fusion = f32[512,896]{1,0:T(8,128)} fusion(bf16[3584,896]{1,0:T(8,128)(2,1)S(1)} %bitcast.112, f32[896]{0:T(1024)S(1)} %convert_element_type.129, bf16[512,3584]{1,0:T(8,128)(2,1)S(1)} %get-tuple-element.12, f32[3584]{0:T(1024)S(1)} %convert_element_type.123, f32[512]{0:T(512)S(1)} %add_rsqrt_fusion), kind=kOutput, calls=%fused_computation.27 | convolution fusion | flops 3296133120 | bytes 11947520 | tf_op jit(solution)/shard_map/dot_general | solution.py:130
  119.3 2.0 copy.40
  124.5 3.0 %copy.53 = f32[512,7,64]{2,0,1:T(8,128)} copy(f32[512,7,64]{0,2,1:T(8,128)} %get-tuple-element.15) | data formatting | bytes 1835008
  127.5 2.0 subtract_convert_fusion
  129.6 2.1 fusion.4
  131.6 2.9 %copy-done.1 = f32[512,512,7]{1,0,2:T(8,128)} copy-done((f32[512,512,7]{1,0,2:T(8,128)}, f32[512,512,7]{1,0,2:T(8,128)S(1)}, u32[]{:S(2)}) %copy-start.1) | copy-done | bytes 7340056
  136.2 7.6 %fusion.12 = bf16[128,7,512]{2,0,1:T(8,128)(2,1)S(1)} fusion(f32[7,512]{1,0:T(8,128)S(1)} %fusion.3, f32[7,512]{1,0:T(8,128)S(1)} %get-tuple-element.26, f32[512,512,7]{1,0,2:T(8,128)} %copy-done.1, pred[512,512]{0,1:T(8,128)(4,1)S(1)} %fusion.21, bf16[3584,128]{1,0:T(8,128)(2,1)S(1)} %copy-done, f32[128]{0:T(128)S(1)} %copy-done.26, ...), kind=kOutput, calls=%fused_computation.28 | convolution fusion | flops 956628992 | bytes 13152768 | tf_op jit(solution)/shard_map/kgqe,ekd->qkgd/dot_general | solution.py:159
  143.8 8.3 %convolution_convert_fusion.1 = bf16[512,3584]{1,0:T(8,128)(2,1)} fusion(bf16[512,896]{0,1:T(8,128)(2,1)S(1)} %bitcast.113, bf16[896,3584]{1,0:T(8,128)(2,1)} %param.32), kind=kOutput, calls=%fused_computation.12 | convolution fusion | flops 3290169344 | bytes 11010048 | tf_op jit(solution)/shard_map/dot_general | solution.py:164
  153.5 3.2 %all-to-all-start.2 = ((f32[2,1,512]{2,1,0:T(1,128)}), f32[2,1,512]{2,1,0:T(1,128)S(1)}, u32[]{:S(2)}, u32[]{:S(2)}) async-start(f32[2,1,512]{2,1,0:T(1,128)} %bitcast.32), calls=%async_computation.3 | async-start | bytes 8192 | tf_op jit(solution)/shard_map/all_to_all | solution.py:106
  158.2 2.2 all-to-all-done.2
  161.4 32.1 %reduce-scatter.2.cloned.1.call-done = bf16[128,3584]{1,0:T(8,128)(2,1)} async-done(((bf16[512,3584]{1,0:T(8,128)(2,1)}), bf16[128,3584]{1,0:T(8,128)(2,1)}) %reduce-scatter.2.cloned.1.call-update) | async-done | bytes 917520 | tf_op jit(solution)/shard_map/reduce_scatter | solution.py:163
  193.5 1.8 fusion.8
  195.4 2.1 fusion.11
  198.7 39.6 %all-reduce = (f32[]{:T(128)}, f32[]{:T(128)}) all-reduce(f32[]{:T(128)} %get-tuple-element.9, f32[]{:T(128)} %get-tuple-element.25), channel_id=1, replica_groups=mesh['row'=2,'col'=4,'mp'=4] {'row','col','mp'}, use_global_device_ids=true, to_apply=%region_15.16 | all-reduce | flops 2 | bytes 16 | tf_op jit(solution)/shard_map/psum | solution.py:190
  (108 shorter events, 20.4 us)
Async XLA Ops:
  7.2 129.0 %copy-start = (bf16[3584,128]{1,0:T(8,128)(2,1)S(1)}, bf16[3584,128]{1,0:T(8,128)(2,1)}, u32[]{:S(2)}) copy-start(bf16[3584,128]{1,0:T(8,128)(2,1)} %param.30) | copy-start | bytes 2752516
  7.2 88.3 %all-gather.2.cloned.1.call-start = ((), (), s32[]{:S(2)}) async-start(), calls=%async_computation.4 | async-start | bytes 9175040 | tf_op jit(solution)/shard_map/all_gather | solution.py:120
  8.8 55.7 %copy-start.16 = (s32[8]{0:T(128)}, s32[8]{0:T(128)S(1)}, u32[]{:S(2)}) copy-start(s32[8]{0:T(128)S(1)} %multiply_add_fusion) | copy-start | bytes 100
  15.4 27.2 %copy-start.20 = (s32[8]{0:T(128)S(1)}, s32[8]{0:T(128)}, u32[]{:S(2)}) copy-start(s32[8]{0:T(128)} %param.24) | copy-start | bytes 100
  15.4 27.2 %copy-start.21 = (f32[8]{0:T(128)S(1)}, f32[8]{0:T(128)}, u32[]{:S(2)}) copy-start(f32[8]{0:T(128)} %param.20) | copy-start | bytes 100
  15.4 48.9 %copy-start.22 = (s32[8]{0:T(128)S(1)}, s32[8]{0:T(128)}, u32[]{:S(2)}) copy-start(s32[8]{0:T(128)} %param.22) | copy-start | bytes 100
  15.4 49.1 %copy-start.23 = (s32[8]{0:T(128)S(1)}, s32[8]{0:T(128)}, u32[]{:S(2)}) copy-start(s32[8]{0:T(128)} %param.23) | copy-start | bytes 100
  15.4 53.2 %copy-start.8 = (bf16[3584]{0:T(1024)(128)(2,1)S(1)}, bf16[3584]{0:T(1024)(128)(2,1)}, u32[]{:S(2)}) copy-start(bf16[3584]{0:T(1024)(128)(2,1)} %param.25) | copy-start | bytes 21508
  15.4 53.2 %copy-start.24 = (bf16[128]{0:T(256)(128)(2,1)S(1)}, bf16[128]{0:T(256)(128)(2,1)}, u32[]{:S(2)}) copy-start(bf16[128]{0:T(256)(128)(2,1)} %param.29) | copy-start | bytes 772
  15.4 53.2 %copy-start.12 = (bf16[896]{0:T(1024)(128)(2,1)S(1)}, bf16[896]{0:T(1024)(128)(2,1)}, u32[]{:S(2)}) copy-start(bf16[896]{0:T(1024)(128)(2,1)} %param.27) | copy-start | bytes 5380
  15.4 53.2 %copy-start.25 = (bf16[128]{0:T(256)(128)(2,1)S(1)}, bf16[128]{0:T(256)(128)(2,1)}, u32[]{:S(2)}) copy-start(bf16[128]{0:T(256)(128)(2,1)} %param.31) | copy-start | bytes 772
  65.3 7.0 %all-to-all-start = ((f32[2,4,3]{1,2,0:T(4,128)}), f32[2,4,3]{1,2,0:T(4,128)S(1)}, u32[]{:S(2)}, u32[]{:S(2)}) async-start(f32[2,4,3]{1,2,0:T(4,128)} %copy.38), calls=%async_computation | async-start | bytes 8192 | tf_op jit(solution)/shard_map/all_to_all | solution.py:107
  68.5 125.0 %reduce-scatter.2.cloned.1.call-start = ((), (), s32[]{:S(2)}) async-start(), calls=%async_computation.5 | async-start | bytes 4587520 | tf_op jit(solution)/shard_map/reduce_scatter | solution.py:163
  74.3 33.3 %copy-start.6 = (pred[512]{0:T(512)(128)(4,1)}, pred[512]{0:T(512)(128)(4,1)S(1)}, u32[]{:S(2)}) copy-start(pred[512]{0:T(512)(128)(4,1)S(1)} %get-tuple-element.23) | copy-start | bytes 1540
  107.6 3.4 %copy-start.19 = (bf16[3584,128]{1,0:T(8,128)(2,1)S(1)}, bf16[3584,128]{1,0:T(8,128)(2,1)}, u32[]{:S(2)}) copy-start(bf16[3584,128]{1,0:T(8,128)(2,1)} %param.28) | copy-start | bytes 2752516
  107.6 6.2 %slice-start = ((s8[6422528]{0:T(1024)(128)(4,1)}), s8[4194304]{0:T(1024)(128)(4,1)S(1)}, s32[]{:S(2)}) async-start(s8[6422528]{0:T(1024)(128)(4,1)} %bitcast.111), calls=%async_computation.6 | async-start | bytes 8388608
  111.0 3.0 %slice-start.1 = ((s8[6422528]{0:T(1024)(128)(4,1)}), s8[2228224]{0:T(1024)(128)(4,1)S(1)}, s32[]{:S(2)}) async-start(s8[6422528]{0:T(1024)(128)(4,1)} %bitcast.111), calls=%async_computation.7 | async-start | bytes 4456448
  131.6 3.0 %copy-start.1 = (f32[512,512,7]{1,0,2:T(8,128)}, f32[512,512,7]{1,0,2:T(8,128)S(1)}, u32[]{:S(2)}) copy-start(f32[512,512,7]{1,0,2:T(8,128)S(1)} %get-tuple-element.27) | copy-start | bytes 22020100
  152.0 4.6 %copy-start.9 = (bf16[3584]{0:T(1024)(128)(2,1)S(1)}, bf16[3584]{0:T(1024)(128)(2,1)}, u32[]{:S(2)}) copy-start(bf16[3584]{0:T(1024)(128)(2,1)} %param.33) | copy-start | bytes 21508
  152.1 5.4 %copy-start.15 = (f32[8]{0:T(128)S(1)}, f32[8]{0:T(128)}, u32[]{:S(2)}) copy-start(f32[8]{0:T(128)} %get-tuple-element.21) | copy-start | bytes 100
  152.1 43.3 %copy-start.3 = (bf16[128,3584]{1,0:T(8,128)(2,1)S(1)}, bf16[128,3584]{1,0:T(8,128)(2,1)}, u32[]{:S(2)}) copy-start(bf16[128,3584]{1,0:T(8,128)(2,1)} %param.34) | copy-start | bytes 2752516
  152.1 45.4 %copy-start.7 = (pred[512]{0:T(512)(128)(4,1)S(1)}, pred[512]{0:T(512)(128)(4,1)}, u32[]{:S(2)}) copy-start(pred[512]{0:T(512)(128)(4,1)} %copy-done.6) | copy-start | bytes 1540
  152.1 45.4 %copy-start.18 = (f32[128]{0:T(128)S(1)}, f32[128]{0:T(128)}, u32[]{:S(2)}) copy-start(f32[128]{0:T(128)} %param.35) | copy-start | bytes 1540
  153.5 7.0 %all-to-all-start.2 = ((f32[2,1,512]{2,1,0:T(1,128)}), f32[2,1,512]{2,1,0:T(1,128)S(1)}, u32[]{:S(2)}, u32[]{:S(2)}) async-start(f32[2,1,512]{2,1,0:T(1,128)} %bitcast.32), calls=%async_computation.3 | async-start | bytes 8192 | tf_op jit(solution)/shard_map/all_to_all | solution.py:106
  (9 other events, 14.7 us)
Sparse Core Ops, SparseCore 0:
  42.7 52.6 all-gather.1
  152.2 41.2 reduce-scatter.1
where the time goes:
time: 248 us
  blocking collectives  87.4 us (35%)
  waiting for transfers between devices  57.4 us (23%)
  local copies, waits for them, and re-layouts  31.4 us (13%)
  matrix products  28.4 us (11%)
  other arithmetic  19.6 us (8%)
  between operations  16.9 us (7%)
  starting transfers between devices  6.51 us (3%)
    psum x1, blocking collectives, body(): lax.psum((jnp.sum(objective), jnp.sum(own_occupied.astype(jnp.float32))),...  39.6 us
    reduce_scatter x1, waiting for transfers between devices, body(): lax.psum_scatter(jnp.dot(pieces, w_out, preferred_element_type=jnp.float3...  32.1 us
    all_to_all x1, blocking collectives, body(): lax.all_to_all(send_rows, 'row', split_axis=0, concat_axis=0, tiled=True)  27.1 us
    psum x1, blocking collectives, body(): lax.psum((jnp.dot(rewards, member, precision=highest), jnp.dot(rewards *...  20.7 us
    all_gather x1, waiting for transfers between devices, body(): all_rows = lax.all_gather(flat_rows, 'mp', axis=1, tiled=True)  20 us
    gather x1, local copies, waits for them, and re-layouts, body(): all_rows[token_index]  12.1 us
    unnamed x60, local copies, waits for them, and re-layouts  9.17 us
    dot_general x1, matrix products, body(): jnp.dot(pieces, w_out, preferred_element_type=jnp.float32)  8.28 us
  transfers between devices with their start and end apart: 4, of which 4 were waited for; matrix products, arithmetic and copies ran while one was open for 3% of the time, Pallas kernels for 0%

commit v1 on v0

--- a/solution.py
+++ b/solution.py
@@ -117,7 +117,9 @@
     positions = jnp.sum(jnp.where(covered, within_all, 0), 1).astype(jnp.float32)
     segment = jnp.where(occupied, jnp.sum(jnp.where(covered, slot_iota[None, :], 0), 1), -1)
     flat_rows = recv_rows.reshape(-1, feature_count)
-    all_rows = lax.all_gather(flat_rows, "mp", axis=1, tiled=True)
+    all_rows = jnp.concatenate(
+        lax.all_to_all(jnp.stack([flat_rows] * lax.axis_size("mp")), "mp", 0, 0), axis=1
+    )
     gathered = jnp.where(occupied[:, None], all_rows[token_index], jnp.zeros((), jnp.bfloat16))
     inverse = lax.rsqrt(
         jnp.mean(jnp.square(gathered.astype(jnp.float32)), -1, keepdims=True) + norm_eps

time: 248 us -> 316 us (1.27)
  waiting for transfers between devices: 57.4 us -> 109 us
  local copies, waits for them, and re-layouts: 31.4 us -> 41.6 us
  starting transfers between devices: 6.51 us -> 12.1 us
  matrix products: 28.4 us -> 32.5 us
  blocking collectives: 87.4 us -> 83.8 us
    all_to_all x0 -> x1, waiting for transfers between devices: none -> 78 us  [body(): lax.all_to_all(jnp.stack([flat_rows] * lax.axis_size('mp')), 'mp', 0, 0)]
    all_gather x1 -> x0, waiting for transfers between devices: 20 us -> none  [body(): all_rows = lax.all_gather(flat_rows, 'mp', axis=1, tiled=True)]
    reshape x0 -> x1, local copies, waits for them, and re-layouts: none -> 6.75 us  [body(): jnp.concatenate(lax.all_to_all(jnp.stack([flat_rows] * lax.axis_size('mp'...]
    all_to_all x1, blocking collectives: 27.1 us -> 21 us  [body(): lax.all_to_all(send_rows, 'row', split_axis=0, concat_axis=0, tiled=True)]
    all_to_all x0 -> x1, starting transfers between devices: none -> 5.6 us  [body(): lax.all_to_all(jnp.stack([flat_rows] * lax.axis_size('mp')), 'mp', 0, 0)]
    reduce_scatter x1, waiting for transfers between devices: 32.1 us -> 28.3 us  [body(): lax.psum_scatter(jnp.dot(pieces, w_out, preferred_element_type=jnp.float3...]
    another operation x0 -> x1, local copies, waits for them, and re-layouts: none -> 3.56 us  [body(): jnp.stack([flat_rows] * lax.axis_size('mp'))]
    unnamed x60 -> x52, local copies, waits for them, and re-layouts: 9.17 us -> 9.16 us
  transfers between devices with their start and end apart: 4 -> 4, of which waited for: 4 -> 3; matrix products, arithmetic and copies ran while one was open for 3% -> 4% of each run, Pallas kernels for 0% -> 0%
where the time goes in v1:
time: 316 us; the launch traced here: 315 us
  waiting for transfers between devices  109 us (34%)
  blocking collectives  83.8 us (27%)
  local copies, waits for them, and re-layouts  41.6 us (13%)
  matrix products  32.5 us (10%)
  other arithmetic  19.5 us (6%)
  between operations  16.9 us (5%)
  starting transfers between devices  12.1 us (4%)
    all_to_all x1, waiting for transfers between devices, body(): lax.all_to_all(jnp.stack([flat_rows] * lax.axis_size('mp')), 'mp', 0, 0)  78 us
    psum x1, blocking collectives, body(): lax.psum((jnp.sum(objective), jnp.sum(own_occupied.astype(jnp.float32))),...  39.5 us
    reduce_scatter x1, waiting for transfers between devices, body(): lax.psum_scatter(jnp.dot(pieces, w_out, preferred_element_type=jnp.float3...  28.3 us
    psum x1, blocking collectives, body(): lax.psum((jnp.dot(rewards, member, precision=highest), jnp.dot(rewards *...  23.3 us
    all_to_all x1, blocking collectives, body(): lax.all_to_all(send_rows, 'row', split_axis=0, concat_axis=0, tiled=True)  21 us
    gather x1, local copies, waits for them, and re-layouts, body(): all_rows[token_index]  12.1 us
    unnamed x52, local copies, waits for them, and re-layouts  9.16 us
    dot_general x1, matrix products, body(): jnp.dot(pieces, w_out, preferred_element_type=jnp.float32)  8.27 us
  transfers between devices with their start and end apart: 4, of which 3 were waited for; matrix products, arithmetic and copies ran while one was open for 4% of the time, Pallas kernels for 0%

profile of v1, /device:TPU:0, one launch (start us, length us, event | category | flops | bytes accessed | tf_op | source)
XLA Modules:
  0.0 314.9 jit_solution(14825513510657635534)
XLA Ops:
  9.0 23.3 %all-reduce.1 = (f32[8]{0:T(128)S(1)}, f32[8]{0:T(128)S(1)}) all-reduce(f32[8]{0:T(128)S(1)} %convolution_bitcast_fusion.2, f32[8]{0:T(128)S(1)} %convolution_bitcast_fusion.4), channel_id=1, replica_groups=mesh['row'=2,'col'=4,'mp'=4] {'row','col'}, use_global_device_ids=true, to_apply=%region_2.3 | all-reduce | flops 16 | bytes 128 | tf_op jit(solution)/shard_map/psum | solution.py:87
  38.1 3.2 %all-to-all-start = ((f32[2,4,3]{1,2,0:T(4,128)}), f32[2,4,3]{1,2,0:T(4,128)S(1)}, u32[]{:S(2)}, u32[]{:S(2)}) async-start(f32[2,4,3]{1,2,0:T(4,128)} %copy.39), calls=%async_computation | async-start | bytes 8192 | tf_op jit(solution)/shard_map/all_to_all | solution.py:107
  41.3 2.3 reshape.264
  45.5 2.3 reshape.265
  47.9 21.0 %all_to_all.24 = bf16[2,512,896]{2,1,0:T(8,128)(2,1)S(1)} all-to-all(bf16[2,512,896]{2,1,0:T(8,128)(2,1)S(1)} %reshape.265), channel_id=1, replica_groups=mesh['row'=2,'col'=4,'mp'=4] {'row'}, dimensions={0} | all-to-all | bytes 3670016 | tf_op jit(solution)/shard_map/all_to_all | solution.py:104
  68.9 3.6 %stack.19 = bf16[4,1024,896]{2,1,0:T(8,128)(2,1)} broadcast(bf16[1024,896]{1,0:T(8,128)(2,1)S(1)} %bitcast.112), dimensions={1,2} | broadcast | bytes 9175040 | tf_op jit(solution)/shard_map/stack | solution.py:121
  72.4 5.6 %all-to-all-start.2 = ((bf16[4,1024,896]{2,1,0:T(8,128)(2,1)}), bf16[4,1024,896]{2,1,0:T(8,128)(2,1)}, u32[]{:S(2)}, u32[]{:S(2)}) async-start(bf16[4,1024,896]{2,1,0:T(8,128)(2,1)} %stack.19), calls=%async_computation.2 | async-start | bytes 14680064 | tf_op jit(solution)/shard_map/all_to_all | solution.py:121
  81.9 78.0 %all-to-all-done.2 = bf16[4,1024,896]{2,1,0:T(8,128)(2,1)} async-done(((bf16[4,1024,896]{2,1,0:T(8,128)(2,1)}), bf16[4,1024,896]{2,1,0:T(8,128)(2,1)}, u32[]{:S(2)}, u32[]{:S(2)}) %all-to-all-start.2) | async-done | bytes 7340064 | tf_op jit(solution)/shard_map/all_to_all | solution.py:121
  159.9 6.7 %copy.56 = bf16[4,128,8,896]{3,2,0,1:T(8,128)(2,1)} copy(bf16[4,128,8,896]{3,2,1,0:T(8,128)(2,1)} %bitcast.39) | data formatting | bytes 14680064 | tf_op jit(solution)/shard_map/reshape | solution.py:120
  166.7 12.1 %gather_fusion = bf16[512,3584]{1,0:T(8,128)(2,1)} fusion(bf16[1024,3584]{1,0:T(8,128)(2,1)} %bitcast.109, s32[1024]{0:T(1024)S(1)} %pad_clamp_fusion.1), kind=kCustom, calls=%fused_computation | custom fusion | bytes 7342080 | tf_op jit(solution)/shard_map/gather | solution.py:123
  178.8 3.4 %fusion = (f32[512]{0:T(512)S(1)}, bf16[512,3584]{1,0:T(8,128)(2,1)S(1)}) fusion(bf16[512,3584]{1,0:T(8,128)(2,1)} %gather_fusion, pred[512]{0:T(512)(128)(4,1)S(1)} %get-tuple-element.23), kind=kLoop, calls=%fused_computation.5 | loop fusion | flops 7339520 | bytes 7342592 | tf_op jit(solution)/shard_map/reduce_sum | solution.py:125
  185.2 5.3 %convolution_add_fusion = f32[512,896]{1,0:T(8,128)} fusion(bf16[3584,896]{1,0:T(8,128)(2,1)S(1)} %bitcast.116, f32[896]{0:T(1024)S(1)} %convert_element_type.129, bf16[512,3584]{1,0:T(8,128)(2,1)S(1)} %get-tuple-element.12, f32[3584]{0:T(1024)S(1)} %convert_element_type.123, f32[512]{0:T(512)S(1)} %add_rsqrt_fusion), kind=kOutput, calls=%fused_computation.27 | convolution fusion | flops 3296133120 | bytes 11947520 | tf_op jit(solution)/shard_map/dot_general | solution.py:132
  190.5 2.0 copy.42
  195.7 3.0 copy.55
  198.7 2.0 subtract_convert_fusion
  200.7 2.1 fusion.4
  202.8 3.0 copy-done.1
  207.4 7.6 %fusion.12 = bf16[128,7,512]{2,0,1:T(8,128)(2,1)S(1)} fusion(f32[7,512]{1,0:T(8,128)S(1)} %fusion.3, f32[7,512]{1,0:T(8,128)S(1)} %get-tuple-element.26, f32[512,512,7]{1,0,2:T(8,128)} %copy-done.1, pred[512,512]{0,1:T(8,128)(4,1)S(1)} %fusion.21, bf16[3584,128]{1,0:T(8,128)(2,1)S(1)} %copy-done, f32[128]{0:T(128)S(1)} %copy-done.22, ...), kind=kOutput, calls=%fused_computation.28 | convolution fusion | flops 956628992 | bytes 13152768 | tf_op jit(solution)/shard_map/kgqe,ekd->qkgd/dot_general | solution.py:161
  215.0 8.3 %convolution_convert_fusion.1 = bf16[512,3584]{1,0:T(8,128)(2,1)} fusion(bf16[512,896]{0,1:T(8,128)(2,1)S(1)} %bitcast.117, bf16[896,3584]{1,0:T(8,128)(2,1)} %param.32), kind=kOutput, calls=%fused_computation.12 | convolution fusion | flops 3290169344 | bytes 11010048 | tf_op jit(solution)/shard_map/dot_general | solution.py:166
  224.6 3.2 %all-to-all-start.3 = ((f32[2,1,512]{2,1,0:T(1,128)}), f32[2,1,512]{2,1,0:T(1,128)S(1)}, u32[]{:S(2)}, u32[]{:S(2)}) async-start(f32[2,1,512]{2,1,0:T(1,128)} %bitcast.33), calls=%async_computation.4 | async-start | bytes 8192 | tf_op jit(solution)/shard_map/all_to_all | solution.py:106
  229.4 2.3 all-to-all-done.3
  232.6 28.3 %reduce-scatter.2.cloned.1.call-done = bf16[128,3584]{1,0:T(8,128)(2,1)} async-done(((bf16[512,3584]{1,0:T(8,128)(2,1)}), bf16[128,3584]{1,0:T(8,128)(2,1)}) %reduce-scatter.2.cloned.1.call-update) | async-done | bytes 917520 | tf_op jit(solution)/shard_map/reduce_scatter | solution.py:165
  262.8 2.1 fusion.11
  266.1 39.5 %all-reduce = (f32[]{:T(128)}, f32[]{:T(128)}) all-reduce(f32[]{:T(128)} %get-tuple-element.9, f32[]{:T(128)} %get-tuple-element.25), channel_id=1, replica_groups=mesh['row'=2,'col'=4,'mp'=4] {'row','col','mp'}, use_global_device_ids=true, to_apply=%region_15.16 | all-reduce | flops 2 | bytes 16 | tf_op jit(solution)/shard_map/psum | solution.py:192
  (101 shorter events, 27.9 us)
Async XLA Ops:
  7.2 200.2 %copy-start = (bf16[3584,128]{1,0:T(8,128)(2,1)S(1)}, bf16[3584,128]{1,0:T(8,128)(2,1)}, u32[]{:S(2)}) copy-start(bf16[3584,128]{1,0:T(8,128)(2,1)} %param.30) | copy-start | bytes 2752516
  35.5 10.0 %copy-start.16 = (s32[8]{0:T(128)}, s32[8]{0:T(128)S(1)}, u32[]{:S(2)}) copy-start(s32[8]{0:T(128)S(1)} %multiply_add_fusion) | copy-start | bytes 100
  38.1 9.8 %all-to-all-start = ((f32[2,4,3]{1,2,0:T(4,128)}), f32[2,4,3]{1,2,0:T(4,128)S(1)}, u32[]{:S(2)}, u32[]{:S(2)}) async-start(f32[2,4,3]{1,2,0:T(4,128)} %copy.39), calls=%async_computation | async-start | bytes 8192 | tf_op jit(solution)/shard_map/all_to_all | solution.py:107
  72.4 5.7 %copy-start.8 = (bf16[3584]{0:T(1024)(128)(2,1)S(1)}, bf16[3584]{0:T(1024)(128)(2,1)}, u32[]{:S(2)}) copy-start(bf16[3584]{0:T(1024)(128)(2,1)} %param.25) | copy-start | bytes 21508
  72.4 5.7 %copy-start.20 = (bf16[128]{0:T(256)(128)(2,1)S(1)}, bf16[128]{0:T(256)(128)(2,1)}, u32[]{:S(2)}) copy-start(bf16[128]{0:T(256)(128)(2,1)} %param.29) | copy-start | bytes 772
  72.4 5.7 %copy-start.12 = (bf16[896]{0:T(1024)(128)(2,1)S(1)}, bf16[896]{0:T(1024)(128)(2,1)}, u32[]{:S(2)}) copy-start(bf16[896]{0:T(1024)(128)(2,1)} %param.27) | copy-start | bytes 5380
  72.4 5.7 %copy-start.21 = (bf16[128]{0:T(256)(128)(2,1)S(1)}, bf16[128]{0:T(256)(128)(2,1)}, u32[]{:S(2)}) copy-start(bf16[128]{0:T(256)(128)(2,1)} %param.31) | copy-start | bytes 772
  72.4 87.5 %all-to-all-start.2 = ((bf16[4,1024,896]{2,1,0:T(8,128)(2,1)}), bf16[4,1024,896]{2,1,0:T(8,128)(2,1)}, u32[]{:S(2)}, u32[]{:S(2)}) async-start(bf16[4,1024,896]{2,1,0:T(8,128)(2,1)} %stack.19), calls=%async_computation.2 | async-start | bytes 14680064 | tf_op jit(solution)/shard_map/all_to_all | solution.py:121
  78.0 182.9 %reduce-scatter.2.cloned.1.call-start = ((), (), s32[]{:S(2)}) async-start(), calls=%async_computation.5 | async-start | bytes 4587520 | tf_op jit(solution)/shard_map/reduce_scatter | solution.py:165
  80.7 98.0 %copy-start.6 = (pred[512]{0:T(512)(128)(4,1)}, pred[512]{0:T(512)(128)(4,1)S(1)}, u32[]{:S(2)}) copy-start(pred[512]{0:T(512)(128)(4,1)S(1)} %get-tuple-element.23) | copy-start | bytes 1540
  178.8 3.4 %copy-start.19 = (bf16[3584,128]{1,0:T(8,128)(2,1)S(1)}, bf16[3584,128]{1,0:T(8,128)(2,1)}, u32[]{:S(2)}) copy-start(bf16[3584,128]{1,0:T(8,128)(2,1)} %param.28) | copy-start | bytes 2752516
  178.8 6.2 %slice-start = ((s8[6422528]{0:T(1024)(128)(4,1)}), s8[4194304]{0:T(1024)(128)(4,1)S(1)}, s32[]{:S(2)}) async-start(s8[6422528]{0:T(1024)(128)(4,1)} %bitcast.115), calls=%async_computation.6 | async-start | bytes 8388608
  182.2 2.8 copy-start.2
  182.2 2.7 copy-start.13
  182.2 3.0 slice-start.1
  198.7 2.0 copy-start.4
  198.7 2.0 copy-start.5
  202.8 3.0 copy-start.1
  223.2 4.6 %copy-start.9 = (bf16[3584]{0:T(1024)(128)(2,1)S(1)}, bf16[3584]{0:T(1024)(128)(2,1)}, u32[]{:S(2)}) copy-start(bf16[3584]{0:T(1024)(128)(2,1)} %param.33) | copy-start | bytes 21508
  223.2 5.4 %copy-start.15 = (f32[8]{0:T(128)S(1)}, f32[8]{0:T(128)}, u32[]{:S(2)}) copy-start(f32[8]{0:T(128)} %get-tuple-element.21) | copy-start | bytes 100
  223.2 39.5 %copy-start.3 = (bf16[128,3584]{1,0:T(8,128)(2,1)S(1)}, bf16[128,3584]{1,0:T(8,128)(2,1)}, u32[]{:S(2)}) copy-start(bf16[128,3584]{1,0:T(8,128)(2,1)} %param.34) | copy-start | bytes 2752516
  223.3 41.6 %copy-start.7 = (pred[512]{0:T(512)(128)(4,1)S(1)}, pred[512]{0:T(512)(128)(4,1)}, u32[]{:S(2)}) copy-start(pred[512]{0:T(512)(128)(4,1)} %copy-done.6) | copy-start | bytes 1540
  223.3 41.6 %copy-start.18 = (f32[128]{0:T(128)S(1)}, f32[128]{0:T(128)}, u32[]{:S(2)}) copy-start(f32[128]{0:T(128)} %param.35) | copy-start | bytes 1540
  224.6 7.0 %all-to-all-start.3 = ((f32[2,1,512]{2,1,0:T(1,128)}), f32[2,1,512]{2,1,0:T(1,128)S(1)}, u32[]{:S(2)}, u32[]{:S(2)}) async-start(f32[2,1,512]{2,1,0:T(1,128)} %bitcast.33), calls=%async_computation.4 | async-start | bytes 8192 | tf_op jit(solution)/shard_map/all_to_all | solution.py:106
  (5 other events, 5.1 us)
Sparse Core Ops, SparseCore 0:
  223.4 37.4 reduce-scatter.1
